TPU v7x, 32 devices: a whole 2x2x4 slice. The times are simulated.
32 devices in a mesh: seg: 4 (over y, x), gx: 2 (over core), gy: 4 (over z).
Axes of the slice: x: 2, y: 2, z: 4, core: 2. Of those that a mesh axis runs over, the one named last changes fastest.
Arguments:
- gas_state: float32 [7, 384, 32, 512], P(None, 'seg', 'gx', 'gy'), may hold values from 0 to 1
- solids_temp: float32 [384, 32, 512], P('seg', 'gx', 'gy'), may hold values from 0.2 to 1.2
- exchange_rate: float32 [32, 512], P('gx', 'gy'), may hold values from 0.1 to 0.5
- column_flags: int32 [32, 512], P('gx', 'gy'), may hold values from 0 to 3
- block_inverse: float32 [384, 96], P('seg'), may hold values from -1 to 2, as said below
- line_coupling: float32 [4, 2], P('seg'), may hold values from 0.05 to 0.25
Outputs:
- gas_next: float32 [7, 384, 32, 512], P(None, 'seg', 'gx', 'gy')
- solids_next: float32 [384, 32, 512], P('seg', 'gx', 'gy')
Inputs may be any that keep to these rules, and one draw needn't show every extreme that they name: `block_inverse`: each block of 96 rows holds the inverse of that segment's diagonal block.
All inputs are finite; a program needn't handle non-finite values.
Results may differ from a plain program's by a relative error of at most 0.000061.
Values sent between devices are 32-bit elements; how exact they have to be, the bound alone decides.
A program may use at most 192 MiB of HBM per device.

v0:
```python
import jax
import jax.numpy as jnp
from jax import lax
from jax.sharding import PartitionSpec as P

diffusion = (0.1, 0.08, 0.12, 0.09, 0.11, 0.07)
stoich = (-1.0, -0.5, 1.0, 0.5, 0.25, 0.75)
rate_const = 0.3
upwind = 0.25
cond_base = 0.04
cond_slope = 0.3
heat_release = 0.5
lateral = 0.1
loss_table = (0.0, 0.3, 0.0, 0.1)
feed_table = (0.0, 0.0, 0.4, 0.0)
highest = lax.Precision.HIGHEST


def with_halo(block, sides, width):
    for axis, dim in sides:
        count = lax.axis_size(axis)
        forward = [(i, i + 1) for i in range(count - 1)]
        backward = [(target, source) for source, target in forward]
        low = lax.ppermute(
            lax.slice_in_dim(block, block.shape[dim] - width, None, axis=dim), axis, forward
        )
        high = lax.ppermute(lax.slice_in_dim(block, 0, width, axis=dim), axis, backward)
        block = jnp.concatenate([low, block, high], axis=dim)
    return block


def advance_species(padded, spread, gains, reaction):
    center = padded[:, 1:-1, 1:-1, 1:-1]
    beside = padded[:, 2:, 1:-1, 1:-1] + padded[:, :-2, 1:-1, 1:-1]
    beside = beside + padded[:, 1:-1, 2:, 1:-1] + padded[:, 1:-1, :-2, 1:-1]
    beside = beside + padded[:, 1:-1, 1:-1, 2:] + padded[:, 1:-1, 1:-1, :-2]
    below = padded[:, :-2, 1:-1, 1:-1]
    return (
        center
        + spread * (beside - 6.0 * center)
        - upwind * (center - below)
        + gains * reaction[None]
    )


def lookup(flags, table):
    result = jnp.zeros(flags.shape, jnp.float32)
    for value, entry in enumerate(table):
        result = result + jnp.where(flags == value, entry, 0.0)
    return result


def advance_enthalpy(heat_pad, mix_pad, reaction, flags):
    cond = cond_base + cond_slope * mix_pad
    heat_mid = heat_pad[1:-1, 1:-1, 1:-1]
    cond_mid = cond[1:-1, 1:-1, 1:-1]
    flux = jnp.zeros(heat_mid.shape, heat_mid.dtype)
    views = (
        (slice(2, None), slice(1, -1), slice(1, -1)),
        (slice(None, -2), slice(1, -1), slice(1, -1)),
        (slice(1, -1), slice(2, None), slice(1, -1)),
        (slice(1, -1), slice(None, -2), slice(1, -1)),
        (slice(1, -1), slice(1, -1), slice(2, None)),
        (slice(1, -1), slice(1, -1), slice(None, -2)),
    )
    for view in views:
        flux = flux + 0.5 * (cond_mid + cond[view]) * (heat_pad[view] - heat_mid)
    loss = lookup(flags, loss_table)[None]
    feed = lookup(flags, feed_table)[None]
    return heat_mid + flux + heat_release * reaction - loss * heat_mid + feed


def solid_source(temp_pad, temp, heat_new, exchange):
    beside = (
        temp_pad[:, 2:, 1:-1]
        + temp_pad[:, :-2, 1:-1]
        + temp_pad[:, 1:-1, 2:]
        + temp_pad[:, 1:-1, :-2]
    )
    return temp + lateral * (beside - 4.0 * temp) + exchange[None] * (heat_new - temp)


def reduced_inverse(scalars):
    count = scalars.shape[0]
    size = 2 * count
    index = jnp.arange(size)
    segment = index // 2
    odd = index % 2
    rows = scalars[segment]
    first = jnp.where(odd == 0, rows[:, 0], rows[:, 1]) * rows[:, 4]
    last = jnp.where(odd == 0, rows[:, 2], rows[:, 3]) * rows[:, 5]
    cols = index[None, :]
    matrix = jnp.eye(size, dtype=scalars.dtype)
    matrix = matrix - jnp.where(cols == (2 * segment - 1)[:, None], first[:, None], 0.0)
    matrix = matrix - jnp.where(cols == (2 * segment + 2)[:, None], last[:, None], 0.0)
    inverse = jnp.eye(size, dtype=scalars.dtype)
    for step in range(size):
        pivot_row = matrix[step] / matrix[step, step]
        pivot_inv = inverse[step] / matrix[step, step]
        is_pivot = index == step
        matrix = jnp.where(is_pivot[:, None], pivot_row[None], matrix)
        inverse = jnp.where(is_pivot[:, None], pivot_inv[None], inverse)
        factor = jnp.where(is_pivot, 0.0, matrix[:, step])
        matrix = matrix - factor[:, None] * pivot_row[None]
        inverse = inverse - factor[:, None] * pivot_inv[None]
    return inverse


def body(gas_state, solids_temp, exchange_rate, column_flags, block_inverse, line_coupling):
    species_count = gas_state.shape[0] - 1
    depth, width_x, width_y = solids_temp.shape
    spread = jnp.array(diffusion, jnp.float32)[:, None, None, None]
    gains = jnp.array(stoich, jnp.float32)[:, None, None, None]
    reaction = rate_const * gas_state[0] * gas_state[1]
    temp_pad = with_halo(solids_temp, (("gx", 1), ("gy", 2)), 1)
    padded = with_halo(gas_state, (("seg", 1), ("gx", 2), ("gy", 3)), 1)
    species_new = advance_species(padded[:species_count], spread, gains, reaction)
    mix = 0.5 * jnp.sum(species_new, axis=0)
    mix_pad = with_halo(mix, (("seg", 0), ("gx", 1), ("gy", 2)), 1)
    heat_pad = padded[species_count]
    heat_new = advance_enthalpy(heat_pad, mix_pad, reaction, column_flags)
    gas_next = jnp.concatenate([species_new, heat_new[None]], axis=0)
    source = solid_source(temp_pad, solids_temp, heat_new, exchange_rate)
    local = jnp.dot(block_inverse, source.reshape(depth, width_x * width_y), precision=highest)
    ends = jnp.stack([local[0], local[depth - 1]])
    scalars = jnp.stack(
        [
            block_inverse[0, 0],
            block_inverse[depth - 1, 0],
            block_inverse[0, depth - 1],
            block_inverse[depth - 1, depth - 1],
            line_coupling[0, 0],
            line_coupling[0, 1],
        ]
    )[None]
    segment_id = lax.axis_index("seg")
    all_ends, all_scalars = (
        lax.all_gather(ends, "seg", axis=0, tiled=True),
        lax.all_gather(scalars, "seg", axis=0, tiled=True),
    )
    inverse = reduced_inverse(all_scalars)
    index = jnp.arange(inverse.shape[0])
    select = jnp.stack([index == 2 * segment_id - 1, index == 2 * segment_id + 2]).astype(
        jnp.float32
    )
    picked = jnp.dot(select, inverse, precision=highest)
    near = jnp.dot(picked, all_ends, precision=highest)
    solved = local + line_coupling[0, 0] * near[0][None, :] * block_inverse[:, 0:1]
    solved = solved + line_coupling[0, 1] * near[1][None, :] * block_inverse[:, depth - 1 : depth]
    return (gas_next, solved.reshape(depth, width_x, width_y))


def solution(mesh):
    in_specs = (
        P(None, "seg", "gx", "gy"),
        P("seg", "gx", "gy"),
        P("gx", "gy"),
        P("gx", "gy"),
        P("seg", None),
        P("seg", None),
    )
    out_specs = (P(None, "seg", "gx", "gy"), P("seg", "gx", "gy"))
    return jax.shard_map(body, mesh=mesh, in_specs=in_specs, out_specs=out_specs, check_vma=False)
```

profile of v0, /device:TPU:0, one launch (start us, length us, event | category | flops | bytes accessed | tf_op | source)
XLA Modules:
  0.0 203.1 jit_solution(5789935153862587755)
XLA Ops:
  0.6 0.9 fusion.64
  1.5 1.3 collective-permute-start
  2.8 6.1 %collective-permute-start.1 = (f32[7,1,16,128]{3,2,1,0:T(8,128)S(1)}, f32[7,1,16,128]{3,2,1,0:T(8,128)}, u32[]{:S(2)}, u32[]{:S(2)}) collective-permute-start(f32[7,1,16,128]{3,2,1,0:T(8,128)S(1)} %get-tuple-element.18), channel_id=1, source_target_pairs={{0,8},{8,16},{16,24},{1,9},{9,17},{17,25},{2,10},{10,18},{18,26},{... | collective-permute-start | bytes 172040 | tf_op jit(solution)/shard_map/ppermute | solution.py:24
  8.9 1.5 copy.47
  10.4 0.7 fusion.66
  11.1 1.3 collective-permute-start.12
  12.3 3.0 %collective-permute-start.13 = (f32[96,1,128]{0,2,1:T(8,128)S(1)}, f32[96,1,128]{0,2,1:T(8,128)S(1)}, u32[]{:S(2)}, u32[]{:S(2)}) collective-permute-start(f32[96,1,128]{0,2,1:T(8,128)S(1)} %get-tuple-element.28), channel_id=1, source_target_pairs={{0,4},{1,5},{2,6},{3,7},{8,12},{9,13},{10,14},{11,15},{16,20},{17,... | collective-permute-start | bytes 147464 | tf_op jit(solution)/shard_map/ppermute | solution.py:24
  15.6 0.7 select_add_fusion
  16.3 1.4 fusion.68
  17.8 1.4 fusion.69
  19.1 1.3 dynamic-slice
  21.0 4.0 %stack.12 = f32[6]{0:T(128)S(1)} concatenate(f32[1]{0:T(128)} %bitcast.7, f32[1]{0:T(128)} %bitcast.8, f32[1]{0:T(128)} %bitcast.9, f32[1]{0:T(128)} %bitcast.10, f32[1]{0:T(128)} %bitcast.11, f32[1]{0:T(128)} %bitcast.12), dimensions={0} | concatenate | bytes 48 | tf_op jit(solution)/shard_map/stack | solution.py:126
  25.2 7.9 %copy.27 = f32[7,96,16,128]{1,3,2,0:T(8,128)} copy(f32[7,96,16,128]{3,2,1,0:T(8,128)} %param.8) | data formatting | bytes 11010048 | tf_op args[0]
  33.1 9.7 %all-reduce = f32[24]{0:T(128)S(1)} all-reduce(f32[24]{0:T(128)S(1)} %dynamic-update-slice), channel_id=2, replica_groups=mesh['seg'=4,'gx'=2,'gy'=4] {'seg'}, use_global_device_ids=true, to_apply=%add | all-reduce | flops 24 | bytes 192
  45.8 0.7 divide_bitcast_fusion.12
  47.3 0.7 divide_bitcast_fusion.13
  61.6 4.5 %copy.29 = f32[7,1,16,128]{1,3,2,0:T(8,128)} copy(f32[7,1,16,128]{3,2,1,0:T(8,128)S(1)} %collective-permute-done) | data formatting | bytes 114688 | tf_op jit(solution)/shard_map/ppermute | solution.py:27
  66.1 5.2 %copy.30 = f32[7,1,16,128]{1,3,2,0:T(8,128)} copy(f32[7,1,16,128]{3,2,1,0:T(8,128)} %collective-permute-done.1) | data formatting | bytes 114688 | tf_op jit(solution)/shard_map/ppermute | solution.py:24
  71.2 2.4 %pad_maximum_fusion.33 = (f32[7,98,1,128]{1,3,2,0:T(8,128)S(1)}, f32[7,98,1,128]{1,3,2,0:T(8,128)S(1)}) fusion(f32[7,1,16,128]{1,3,2,0:T(8,128)} %copy.29, f32[7,96,16,128]{1,3,2,0:T(8,128)} %copy.27, f32[7,1,16,128]{1,3,2,0:T(8,128)} %copy.30), kind=kLoop, calls=%fused_computation.92 | loop fusion | flops 351232 | bytes 6322176 | tf_op jit(solution)/shard_map/concatenate | solution.py:28
  73.7 1.6 collective-permute-start.2
  75.2 3.1 %collective-permute-start.3 = (f32[7,98,1,128]{1,3,2,0:T(8,128)S(1)}, f32[7,98,1,128]{1,3,2,0:T(8,128)S(1)}, u32[]{:S(2)}, u32[]{:S(2)}) collective-permute-start(f32[7,98,1,128]{1,3,2,0:T(8,128)S(1)} %get-tuple-element.16), channel_id=1, source_target_pairs={{0,4},{1,5},{2,6},{3,7},{8,12},{9,13},{10,14},{11,15},{16,20},{17,... | collective-permute-start | bytes 1053704 | tf_op jit(solution)/shard_map/ppermute | solution.py:24
  78.4 1.1 fusion.40
  79.7 1.9 pad_maximum_fusion.39
  81.6 1.3 collective-permute-start.4
  82.9 4.7 %collective-permute-start.5 = (f32[7,98,18,1]{1,3,2,0:T(1,128)S(1)}, f32[7,98,18,1]{1,3,2,0:T(1,128)S(1)}, u32[]{:S(2)}, u32[]{:S(2)}) collective-permute-start(f32[7,98,18,1]{1,3,2,0:T(1,128)S(1)} %get-tuple-element.14), channel_id=1, source_target_pairs={{0,1},{1,2},{2,3},{4,5},{5,6},{6,7},{8,9},{9,10},{10,11},{12,13},{... | collective-permute-start | bytes 148184 | tf_op jit(solution)/shard_map/ppermute | solution.py:24
  87.7 0.8 fusion.44
  88.4 0.9 collective-permute-done.5
  89.4 48.4 %fusion.62 = (f32[96,16,128]{0,2,1:T(8,128)S(1)}, f32[6,96,16,128]{1,3,2,0:T(8,128)}) fusion(f32[96,16,128]{0,2,1:T(8,128)} %fusion.40, f32[6]{0:T(128)S(1)} %copy-done.13, f32[7,98,1,128]{1,3,2,0:T(8,128)} %copy-done.3, f32[7,1,16,128]{1,3,2,0:T(8,128)} %copy.29, f32[7,96,16,128]{1,3,2,0:T(8,128)} %copy.27, f32[7,1,16,128]{1,3,2,0:T(8,128)} %copy.30, ...), kind=kLoop, calls=%fused_computation.222 | loop fusion | flops 38731776 | bytes 35881488 | tf_op jit(solution)/shard_map/reduce_sum | solution.py:118
  138.6 1.7 collective-permute-start.6
  140.6 1.3 collective-permute-start.7
  141.9 0.7 slice_reduce_fusion.1
  143.0 4.3 %collective-permute-done.7 = f32[1,16,128]{2,1,0:T(8,128)S(1)} collective-permute-done((f32[1,16,128]{2,1,0:T(8,128)S(1)}, f32[1,16,128]{2,1,0:T(8,128)S(1)}, u32[]{:S(2)}, u32[]{:S(2)}) %collective-permute-start.7) | collective-permute-done | bytes 8224 | tf_op jit(solution)/shard_map/ppermute | solution.py:27
  147.9 1.4 collective-permute-start.8
  149.3 1.3 collective-permute-start.9
  150.6 0.9 pad_maximum_fusion.46
  151.5 1.3 collective-permute-start.14
  152.8 4.9 %collective-permute-start.15 = (f32[96,18,1]{0,2,1:T(1,128)S(1)}, f32[96,18,1]{0,2,1:T(1,128)S(1)}, u32[]{:S(2)}, u32[]{:S(2)}) collective-permute-start(f32[96,18,1]{0,2,1:T(1,128)S(1)} %get-tuple-element.25), channel_id=1, source_target_pairs={{0,1},{1,2},{2,3},{4,5},{5,6},{6,7},{8,9},{9,10},{10,11},{12,13},{... | collective-permute-start | bytes 20744 | tf_op jit(solution)/shard_map/ppermute | solution.py:24
  157.9 3.9 %collective-permute-start.10 = (f32[98,18,1]{0,2,1:T(1,128)S(1)}, f32[98,18,1]{0,2,1:T(1,128)S(1)}, u32[]{:S(2)}, u32[]{:S(2)}) collective-permute-start(f32[98,18,1]{0,2,1:T(1,128)S(1)} %get-tuple-element.20), channel_id=1, source_target_pairs={{0,1},{1,2},{2,3},{4,5},{5,6},{6,7},{8,9},{9,10},{10,11},{12,13},{... | collective-permute-start | bytes 21176 | tf_op jit(solution)/shard_map/ppermute | solution.py:24
  161.8 1.6 collective-permute-start.11
  163.5 2.5 %fusion.10 = f32[98,18,130]{0,2,1:T(8,128)S(1)} fusion(f32[7,98,18,1]{1,3,2,0:T(1,128)S(1)} %collective-permute-done.4, f32[7,98,18,1]{1,3,2,0:T(1,128)S(1)} %collective-permute-done.5, f32[7,98,1,128]{1,3,2,0:T(8,128)S(1)} %copy-done.4, f32[7,98,1,128]{1,3,2,0:T(8,128)S(1)} %copy-done.6, f32[7,1,16,128]{1,3,2,0:T(8,128)} %copy.29, ...), kind=kLoop, calls=%fused_computation.32 | loop fusion | flops 1375920 | bytes 7338240 | tf_op jit(solution)/shard_map/squeeze | solution.py:120
  166.0 1.5 collective-permute-done.11
  168.2 6.2 %fusion.16 = (f32[96,16,128]{0,2,1:T(8,128)S(1)}, f32[96,16,128]{0,2,1:T(8,128)S(1)}) fusion(f32[96,16,128]{0,2,1:T(8,128)S(1)} %copy-done.2, f32[96,18,1]{0,2,1:T(1,128)S(1)} %collective-permute-done.15, f32[96,1,128]{0,2,1:T(8,128)S(1)} %collective-permute-done.12, f32[96,1,128]{0,2,1:T(8,128)S(1)} %collective-permute-done.13, ...), kind=kLoop, calls=%fused_computation.45 | loop fusion | flops 10813440 | bytes 15078912 | tf_op jit(solution)/shard_map/add | solution.py:80
  174.5 1.2 convolution_bitcast_fusion
  175.7 9.6 %all-gather.1 = f32[4,2,2048]{2,1,0:T(2,128)S(1)} all-gather(f32[1,2,2048]{2,1,0:T(2,128)S(1)} %maximum_bitcast_fusion), channel_id=1, replica_groups=mesh['seg'=4,'gx'=2,'gy'=4] {'seg'}, dimensions={0}, use_global_device_ids=true | all-gather | bytes 81920 | tf_op jit(solution)/shard_map/all_gather | solution.py:138
  185.6 1.3 slice_multiply_fusion.3
  187.1 1.0 copy.50
  188.1 7.0 %pad_maximum_fusion = f32[7,96,16,128]{1,3,2,0:T(8,128)} fusion(f32[1,96,16,128]{1,3,2,0:T(8,128)S(1)} %bitcast.73, f32[6,96,16,128]{1,3,2,0:T(8,128)} %get-tuple-element.13), kind=kLoop, calls=%fused_computation.1 | loop fusion | flops 1376256 | bytes 11010048 | tf_op jit(solution)/shard_map/concatenate | solution.py:122
  195.2 7.9 %copy.49 = f32[7,96,16,128]{3,2,1,0:T(8,128)} copy(f32[7,96,16,128]{1,3,2,0:T(8,128)} %pad_maximum_fusion) | data formatting | bytes 11010048
  (123 shorter events, 21.2 us)
Async XLA Ops:
  1.5 60.1 %collective-permute-start = (f32[7,1,16,128]{3,2,1,0:T(8,128)S(1)}, f32[7,1,16,128]{3,2,1,0:T(8,128)S(1)}, u32[]{:S(2)}, u32[]{:S(2)}) collective-permute-start(f32[7,1,16,128]{3,2,1,0:T(8,128)S(1)} %get-tuple-element.19), channel_id=1, source_target_pairs={{8,0},{16,8},{24,16},{9,1},{17,9},{25,17},{10,2},{18,10},{26,18},{... | collective-permute-start | bytes 172040 | tf_op jit(solution)/shard_map/ppermute | solution.py:27
  2.8 63.3 %collective-permute-start.1 = (f32[7,1,16,128]{3,2,1,0:T(8,128)S(1)}, f32[7,1,16,128]{3,2,1,0:T(8,128)}, u32[]{:S(2)}, u32[]{:S(2)}) collective-permute-start(f32[7,1,16,128]{3,2,1,0:T(8,128)S(1)} %get-tuple-element.18), channel_id=1, source_target_pairs={{0,8},{8,16},{16,24},{1,9},{9,17},{17,25},{2,10},{10,18},{18,26},{... | collective-permute-start | bytes 172040 | tf_op jit(solution)/shard_map/ppermute | solution.py:24
  10.4 22.7 %copy-start.1 = (f32[96,16,128]{0,2,1:T(8,128)}, f32[96,16,128]{0,2,1:T(8,128)S(1)}, u32[]{:S(2)}) copy-start(f32[96,16,128]{0,2,1:T(8,128)S(1)} %copy.47) | copy-start | bytes 2359300
  11.1 139.5 %collective-permute-start.12 = (f32[96,1,128]{0,2,1:T(8,128)}, f32[96,1,128]{0,2,1:T(8,128)S(1)}, u32[]{:S(2)}, u32[]{:S(2)}) collective-permute-start(f32[96,1,128]{0,2,1:T(8,128)} %get-tuple-element.29), channel_id=1, source_target_pairs={{4,0},{5,1},{6,2},{7,3},{12,8},{13,9},{14,10},{15,11},{20,16},{21,... | collective-permute-start | bytes 147464 | tf_op jit(solution)/shard_map/ppermute | solution.py:27
  12.3 138.3 %collective-permute-start.13 = (f32[96,1,128]{0,2,1:T(8,128)S(1)}, f32[96,1,128]{0,2,1:T(8,128)S(1)}, u32[]{:S(2)}, u32[]{:S(2)}) collective-permute-start(f32[96,1,128]{0,2,1:T(8,128)S(1)} %get-tuple-element.28), channel_id=1, source_target_pairs={{0,4},{1,5},{2,6},{3,7},{8,12},{9,13},{10,14},{11,15},{16,20},{17,... | collective-permute-start | bytes 147464 | tf_op jit(solution)/shard_map/ppermute | solution.py:24
  66.1 12.3 %slice-start = ((s8[7340032]{0:T(1024)(128)(4,1)}), s8[3145728]{0:T(1024)(128)(4,1)S(1)}, s32[]{:S(2)}) async-start(s8[7340032]{0:T(1024)(128)(4,1)} %bitcast.71), calls=%async_computation | async-start | bytes 6291456
  71.2 7.1 %slice-start.1 = ((s8[7340032]{0:T(1024)(128)(4,1)}), s8[4194304]{0:T(1024)(128)(4,1)S(1)}, s32[]{:S(2)}) async-start(s8[7340032]{0:T(1024)(128)(4,1)} %bitcast.71), calls=%async_computation.1 | async-start | bytes 8388608
  71.2 8.5 %copy-start = (f32[7,1,16,128]{1,3,2,0:T(8,128)S(1)}, f32[7,1,16,128]{1,3,2,0:T(8,128)}, u32[]{:S(2)}) copy-start(f32[7,1,16,128]{1,3,2,0:T(8,128)} %copy.30) | copy-start | bytes 172036
  73.7 5.8 %collective-permute-start.2 = (f32[7,98,1,128]{1,3,2,0:T(8,128)S(1)}, f32[7,98,1,128]{1,3,2,0:T(8,128)S(1)}, u32[]{:S(2)}, u32[]{:S(2)}) collective-permute-start(f32[7,98,1,128]{1,3,2,0:T(8,128)S(1)} %get-tuple-element.17), channel_id=1, source_target_pairs={{4,0},{5,1},{6,2},{7,3},{12,8},{13,9},{14,10},{15,11},{20,16},{21,... | collective-permute-start | bytes 1053704 | tf_op jit(solution)/shard_map/ppermute | solution.py:27
  75.2 4.5 %collective-permute-start.3 = (f32[7,98,1,128]{1,3,2,0:T(8,128)S(1)}, f32[7,98,1,128]{1,3,2,0:T(8,128)S(1)}, u32[]{:S(2)}, u32[]{:S(2)}) collective-permute-start(f32[7,98,1,128]{1,3,2,0:T(8,128)S(1)} %get-tuple-element.16), channel_id=1, source_target_pairs={{0,4},{1,5},{2,6},{3,7},{8,12},{9,13},{10,14},{11,15},{16,20},{17,... | collective-permute-start | bytes 1053704 | tf_op jit(solution)/shard_map/ppermute | solution.py:24
  79.5 9.9 %copy-start.12 = (f32[6]{0:T(128)S(1)}, f32[6]{0:T(128)}, u32[]{:S(2)}) copy-start(f32[6]{0:T(128)} %constant.83.clone) | copy-start | bytes 76
  79.5 9.9 %copy-start.13 = (f32[6]{0:T(128)S(1)}, f32[6]{0:T(128)}, u32[]{:S(2)}) copy-start(f32[6]{0:T(128)} %constant.84.clone) | copy-start | bytes 76
  79.5 2.1 %copy-start.3 = (f32[7,98,1,128]{1,3,2,0:T(8,128)}, f32[7,98,1,128]{1,3,2,0:T(8,128)S(1)}, u32[]{:S(2)}) copy-start(f32[7,98,1,128]{1,3,2,0:T(8,128)S(1)} %collective-permute-done.2) | copy-start | bytes 1053700
  79.7 1.9 copy-start.5
  81.6 6.8 %collective-permute-start.4 = (f32[7,98,18,1]{1,3,2,0:T(1,128)S(1)}, f32[7,98,18,1]{1,3,2,0:T(1,128)S(1)}, u32[]{:S(2)}, u32[]{:S(2)}) collective-permute-start(f32[7,98,18,1]{1,3,2,0:T(1,128)S(1)} %get-tuple-element.15), channel_id=1, source_target_pairs={{1,0},{2,1},{3,2},{5,4},{6,5},{7,6},{9,8},{10,9},{11,10},{13,12},{... | collective-permute-start | bytes 148184 | tf_op jit(solution)/shard_map/ppermute | solution.py:27
  82.9 6.4 %collective-permute-start.5 = (f32[7,98,18,1]{1,3,2,0:T(1,128)S(1)}, f32[7,98,18,1]{1,3,2,0:T(1,128)S(1)}, u32[]{:S(2)}, u32[]{:S(2)}) collective-permute-start(f32[7,98,18,1]{1,3,2,0:T(1,128)S(1)} %get-tuple-element.14), channel_id=1, source_target_pairs={{0,1},{1,2},{2,3},{4,5},{5,6},{6,7},{8,9},{9,10},{10,11},{12,13},{... | collective-permute-start | bytes 148184 | tf_op jit(solution)/shard_map/ppermute | solution.py:24
  137.8 4.1 %copy-start.7 = (f32[96,96]{1,0:T(8,128)S(1)}, f32[96,96]{1,0:T(8,128)}, u32[]{:S(2)}) copy-start(f32[96,96]{1,0:T(8,128)} %param.12) | copy-start | bytes 110596
  138.6 4.0 %collective-permute-start.6 = (f32[1,16,128]{2,1,0:T(8,128)S(1)}, f32[1,16,128]{2,1,0:T(8,128)S(1)}, u32[]{:S(2)}, u32[]{:S(2)}) collective-permute-start(f32[1,16,128]{2,1,0:T(8,128)S(1)} %copy.37), channel_id=1, source_target_pairs={{0,8},{8,16},{16,24},{1,9},{9,17},{17,25},{2,10},{10,18},{18,26},{... | collective-permute-start | bytes 24584 | tf_op jit(solution)/shard_map/ppermute | solution.py:24
  140.6 6.7 %collective-permute-start.7 = (f32[1,16,128]{2,1,0:T(8,128)S(1)}, f32[1,16,128]{2,1,0:T(8,128)S(1)}, u32[]{:S(2)}, u32[]{:S(2)}) collective-permute-start(f32[1,16,128]{2,1,0:T(8,128)S(1)} %copy.38), channel_id=1, source_target_pairs={{8,0},{16,8},{24,16},{9,1},{17,9},{25,17},{10,2},{18,10},{26,18},{... | collective-permute-start | bytes 24584 | tf_op jit(solution)/shard_map/ppermute | solution.py:27
  147.7 15.8 %copy-start.4 = (f32[7,98,1,128]{1,3,2,0:T(8,128)S(1)}, f32[7,98,1,128]{1,3,2,0:T(8,128)}, u32[]{:S(2)}) copy-start(f32[7,98,1,128]{1,3,2,0:T(8,128)} %copy-done.3) | copy-start | bytes 1053700
  147.7 15.8 %copy-start.6 = (f32[7,98,1,128]{1,3,2,0:T(8,128)S(1)}, f32[7,98,1,128]{1,3,2,0:T(8,128)}, u32[]{:S(2)}) copy-start(f32[7,98,1,128]{1,3,2,0:T(8,128)} %copy-done.5) | copy-start | bytes 1053700
  147.9 9.9 %collective-permute-start.8 = (f32[98,1,128]{0,2,1:T(8,128)S(1)}, f32[98,1,128]{0,2,1:T(8,128)S(1)}, u32[]{:S(2)}, u32[]{:S(2)}) collective-permute-start(f32[98,1,128]{0,2,1:T(8,128)S(1)} %get-tuple-element.22), channel_id=1, source_target_pairs={{0,4},{1,5},{2,6},{3,7},{8,12},{9,13},{10,14},{11,15},{16,20},{17,... | collective-permute-start | bytes 150536 | tf_op jit(solution)/shard_map/ppermute | solution.py:24
  149.3 8.4 %collective-permute-start.9 = (f32[98,1,128]{0,2,1:T(8,128)S(1)}, f32[98,1,128]{0,2,1:T(8,128)S(1)}, u32[]{:S(2)}, u32[]{:S(2)}) collective-permute-start(f32[98,1,128]{0,2,1:T(8,128)S(1)} %get-tuple-element.23), channel_id=1, source_target_pairs={{4,0},{5,1},{6,2},{7,3},{12,8},{13,9},{14,10},{15,11},{20,16},{21,... | collective-permute-start | bytes 150536 | tf_op jit(solution)/shard_map/ppermute | solution.py:27
  151.5 16.7 %collective-permute-start.14 = (f32[96,18,1]{0,2,1:T(1,128)S(1)}, f32[96,18,1]{0,2,1:T(1,128)S(1)}, u32[]{:S(2)}, u32[]{:S(2)}) collective-permute-start(f32[96,18,1]{0,2,1:T(1,128)S(1)} %get-tuple-element.24), channel_id=1, source_target_pairs={{1,0},{2,1},{3,2},{5,4},{6,5},{7,6},{9,8},{10,9},{11,10},{13,12},{... | collective-permute-start | bytes 20744 | tf_op jit(solution)/shard_map/ppermute | solution.py:27
  152.8 15.4 %collective-permute-start.15 = (f32[96,18,1]{0,2,1:T(1,128)S(1)}, f32[96,18,1]{0,2,1:T(1,128)S(1)}, u32[]{:S(2)}, u32[]{:S(2)}) collective-permute-start(f32[96,18,1]{0,2,1:T(1,128)S(1)} %get-tuple-element.25), channel_id=1, source_target_pairs={{0,1},{1,2},{2,3},{4,5},{5,6},{6,7},{8,9},{9,10},{10,11},{12,13},{... | collective-permute-start | bytes 20744 | tf_op jit(solution)/shard_map/ppermute | solution.py:24
  157.9 8.1 %collective-permute-start.10 = (f32[98,18,1]{0,2,1:T(1,128)S(1)}, f32[98,18,1]{0,2,1:T(1,128)S(1)}, u32[]{:S(2)}, u32[]{:S(2)}) collective-permute-start(f32[98,18,1]{0,2,1:T(1,128)S(1)} %get-tuple-element.20), channel_id=1, source_target_pairs={{0,1},{1,2},{2,3},{4,5},{5,6},{6,7},{8,9},{9,10},{10,11},{12,13},{... | collective-permute-start | bytes 21176 | tf_op jit(solution)/shard_map/ppermute | solution.py:24
  161.8 6.4 %copy-start.2 = (f32[96,16,128]{0,2,1:T(8,128)S(1)}, f32[96,16,128]{0,2,1:T(8,128)}, u32[]{:S(2)}) copy-start(f32[96,16,128]{0,2,1:T(8,128)} %copy-done.1) | copy-start | bytes 2359300
  161.8 6.4 %copy-start.8 = (f32[16,128]{1,0:T(8,128)S(1)}, f32[16,128]{1,0:T(8,128)}, u32[]{:S(2)}) copy-start(f32[16,128]{1,0:T(8,128)} %param.10) | copy-start | bytes 24580
  161.8 5.7 %collective-permute-start.11 = (f32[98,18,1]{0,2,1:T(1,128)S(1)}, f32[98,18,1]{0,2,1:T(1,128)S(1)}, u32[]{:S(2)}, u32[]{:S(2)}) collective-permute-start(f32[98,18,1]{0,2,1:T(1,128)S(1)} %get-tuple-element.21), channel_id=1, source_target_pairs={{1,0},{2,1},{3,2},{5,4},{6,5},{7,6},{9,8},{10,9},{11,10},{13,12},{... | collective-permute-start | bytes 21176 | tf_op jit(solution)/shard_map/ppermute | solution.py:27
  168.2 17.2 %copy-start.11 = (f32[2,8]{1,0:T(2,128)S(1)}, f32[2,8]{1,0:T(2,128)}, u32[]{:S(2)}) copy-start(f32[2,8]{1,0:T(2,128)} %fusion.44) | copy-start | bytes 196
  168.2 18.7 %copy-start.9 = (f32[96]{0:T(128)S(1)}, f32[96]{0:T(128)}, u32[]{:S(2)}) copy-start(f32[96]{0:T(128)} %get-tuple-element.6) | copy-start | bytes 1156
  168.2 18.7 %copy-start.10 = (f32[96]{0:T(128)S(1)}, f32[96]{0:T(128)}, u32[]{:S(2)}) copy-start(f32[96]{0:T(128)} %get-tuple-element.7) | copy-start | bytes 1156
where the time goes:
time: 204 us; the launch traced here: 203 us
  other arithmetic  87.1 us (43%)
  local copies, waits for them, and re-layouts  45.7 us (22%)
  starting transfers between devices  39.8 us (20%)
  blocking collectives  19.4 us (10%)
  waiting for transfers between devices  6.94 us (3%)
  matrix products  2.19 us (1%)
    reduce_sum x1, other arithmetic, body(): mix = 0.5 * jnp.sum(species_new, axis=0)  48.4 us
    ppermute x8, starting transfers between devices, with_halo(): lax.ppermute(lax.slice_in_dim(block, block.shape[dim] - width, None, axis...  28.9 us
    unnamed x40, local copies, waits for them, and re-layouts  19.9 us
    ppermute x8, starting transfers between devices, with_halo(): lax.ppermute(lax.slice_in_dim(block, 0, width, axis=dim), axis, backward)  10.9 us
    unnamed x1, blocking collectives  9.74 us
    all_gather x1, blocking collectives, body(): lax.all_gather(ends, 'seg', axis=0, tiled=True)  9.64 us
    concatenate x1, other arithmetic, body(): gas_next = jnp.concatenate([species_new, heat_new[None]], axis=0)  7.02 us
    add x1, other arithmetic, solid_source(): temp + lateral * (beside - 4.0 * temp) + exchange[None] * (heat_new - temp)  6.22 us
  transfers between devices with their start and end apart: 16, of which 4 were waited for; matrix products, arithmetic and copies ran while one was open for 54% of the time, Pallas kernels for 0%

commit v1 on v0

--- a/solution.py
+++ b/solution.py
@@ -14,6 +14,24 @@
 loss_table = (0.0, 0.3, 0.0, 0.1)
 feed_table = (0.0, 0.0, 0.4, 0.0)
 highest = lax.Precision.HIGHEST
+
+
+def ring_gather(value, axis, dim):
+    ways, here, step = (lax.axis_size(axis), lax.axis_index(axis), value.shape[dim])
+    lengths = [n * ways if d == dim else n for d, n in enumerate(value.shape)]
+    full = lax.dynamic_update_slice_in_dim(
+        jnp.zeros(lengths, value.dtype), value, here * step, axis=dim
+    )
+    going_up = going_down = value
+    for far in range(1, ways // 2 + 1):
+        going_up = lax.ppermute(going_up, axis, [(d, (d + 1) % ways) for d in range(ways)])
+        full = lax.dynamic_update_slice_in_dim(full, going_up, (here - far) % ways * step, axis=dim)
+        if 2 * far < ways:
+            going_down = lax.ppermute(going_down, axis, [(d, (d - 1) % ways) for d in range(ways)])
+            full = lax.dynamic_update_slice_in_dim(
+                full, going_down, (here + far) % ways * step, axis=dim
+            )
+    return full
 
 
 def with_halo(block, sides, width):
@@ -135,7 +153,7 @@
     )[None]
     segment_id = lax.axis_index("seg")
     all_ends, all_scalars = (
-        lax.all_gather(ends, "seg", axis=0, tiled=True),
+        ring_gather(ends, "seg", 0),
         lax.all_gather(scalars, "seg", axis=0, tiled=True),
     )
     inverse = reduced_inverse(all_scalars)

time: 204 us -> 196 us (0.961)
  blocking collectives: 19.4 us -> 9.74 us
  starting transfers between devices: 39.8 us -> 44.9 us
  other arithmetic: 87.1 us -> 82.9 us
  waiting for transfers between devices: 6.94 us -> 9.55 us
  local copies, waits for them, and re-layouts: 45.7 us -> 43.4 us
    all_gather x1 -> x0, blocking collectives: 9.64 us -> none  [body(): lax.all_gather(ends, 'seg', axis=0, tiled=True)]
    ppermute x0 -> x3, starting transfers between devices: none -> 4.99 us  [the longest x2 4.98 us: ring_gather(): lax.ppermute(going_up, axis, [(d, (d + 1) % ways) for d in range(ways)])]
    concatenate x1, other arithmetic: 7.02 us -> 3.8 us  [body(): gas_next = jnp.concatenate([species_new, heat_new[None]], axis=0)]
    ppermute x0 -> x3, waiting for transfers between devices: none -> 2.59 us  [the longest x2 2.58 us: ring_gather(): lax.ppermute(going_up, axis, [(d, (d + 1) % ways) for d in range(ways)])]
    unnamed x40 -> x49, local copies, waits for them, and re-layouts: 19.9 us -> 19.2 us
  transfers between devices with their start and end apart: 16 -> 19, of which waited for: 4 -> 5; matrix products, arithmetic and copies ran while one was open for 54% -> 60% of each run, Pallas kernels for 0% -> 0%
where the time goes in v1:
time: 196 us; the launch traced here: 195 us
  other arithmetic  82.9 us (42%)
  starting transfers between devices  44.9 us (23%)
  local copies, waits for them, and re-layouts  43.4 us (22%)
  blocking collectives  9.74 us (5%)
  waiting for transfers between devices  9.55 us (5%)
  matrix products  2.2 us (1%)
    reduce_sum x1, other arithmetic, body(): mix = 0.5 * jnp.sum(species_new, axis=0)  47.5 us
    ppermute x8, starting transfers between devices, with_halo(): lax.ppermute(lax.slice_in_dim(block, block.shape[dim] - width, None, axis...  29 us
    unnamed x49, local copies, waits for them, and re-layouts  19.2 us
    ppermute x8, starting transfers between devices, with_halo(): lax.ppermute(lax.slice_in_dim(block, 0, width, axis=dim), axis, backward)  10.9 us
    unnamed x1, blocking collectives  9.74 us
    add x1, other arithmetic, solid_source(): temp + lateral * (beside - 4.0 * temp) + exchange[None] * (heat_new - temp)  6.37 us
    broadcast_in_dim x8, other arithmetic, reduced_inverse(): inverse = jnp.where(is_pivot[:, None], pivot_inv[None], inverse)  5.85 us
    ppermute x8, waiting for transfers between devices, with_halo(): lax.ppermute(lax.slice_in_dim(block, 0, width, axis=dim), axis, backward)  5.84 us
  transfers between devices with their start and end apart: 19, of which 5 were waited for; matrix products, arithmetic and copies ran while one was open for 60% of the time, Pallas kernels for 0%

profile of v1, /device:TPU:0, one launch (start us, length us, event | category | flops | bytes accessed | tf_op | source)
XLA Modules:
  0.0 194.6 jit_solution(2337731595085878039)
XLA Ops:
  0.6 0.9 fusion.64
  1.5 1.3 collective-permute-start
  2.8 6.1 %collective-permute-start.1 = (f32[7,1,16,128]{3,2,1,0:T(8,128)S(1)}, f32[7,1,16,128]{3,2,1,0:T(8,128)}, u32[]{:S(2)}, u32[]{:S(2)}) collective-permute-start(f32[7,1,16,128]{3,2,1,0:T(8,128)S(1)} %get-tuple-element.18), channel_id=1, source_target_pairs={{0,8},{8,16},{16,24},{1,9},{9,17},{17,25},{2,10},{10,18},{18,26},{... | collective-permute-start | bytes 172040 | tf_op jit(solution)/shard_map/ppermute | solution.py:42
  8.9 1.5 copy.47
  10.4 0.7 fusion.66
  11.1 1.3 collective-permute-start.12
  12.4 3.2 %collective-permute-start.13 = (f32[96,1,128]{0,2,1:T(8,128)S(1)}, f32[96,1,128]{0,2,1:T(8,128)S(1)}, u32[]{:S(2)}, u32[]{:S(2)}) collective-permute-start(f32[96,1,128]{0,2,1:T(8,128)S(1)} %get-tuple-element.28), channel_id=1, source_target_pairs={{0,4},{1,5},{2,6},{3,7},{8,12},{9,13},{10,14},{11,15},{16,20},{17,... | collective-permute-start | bytes 147464 | tf_op jit(solution)/shard_map/ppermute | solution.py:42
  15.6 7.9 %copy.27 = f32[7,96,16,128]{1,3,2,0:T(8,128)} copy(f32[7,96,16,128]{3,2,1,0:T(8,128)} %param.8) | data formatting | bytes 11010048 | tf_op args[0]
  26.1 3.8 %stack.12 = f32[6]{0:T(128)S(1)} concatenate(f32[1]{0:T(128)} %bitcast.7, f32[1]{0:T(128)} %bitcast.8, f32[1]{0:T(128)} %bitcast.9, f32[1]{0:T(128)} %bitcast.10, f32[1]{0:T(128)} %bitcast.11, f32[1]{0:T(128)} %bitcast.12), dimensions={0} | concatenate | bytes 48 | tf_op jit(solution)/shard_map/stack | solution.py:144
  30.2 9.7 %all-reduce = f32[24]{0:T(128)S(1)} all-reduce(f32[24]{0:T(128)S(1)} %dynamic-update-slice), channel_id=2, replica_groups=mesh['seg'=4,'gx'=2,'gy'=4] {'seg'}, use_global_device_ids=true, to_apply=%add | all-reduce | flops 24 | bytes 192
  42.3 0.7 slice.381
  42.9 0.7 divide_bitcast_fusion.12
  44.4 0.7 divide_bitcast_fusion.13
  57.8 1.2 divide_bitcast_fusion.1
  59.3 4.5 %copy.29 = f32[7,1,16,128]{1,3,2,0:T(8,128)} copy(f32[7,1,16,128]{3,2,1,0:T(8,128)S(1)} %collective-permute-done) | data formatting | bytes 114688 | tf_op jit(solution)/shard_map/ppermute | solution.py:45
  63.8 5.2 %copy.30 = f32[7,1,16,128]{1,3,2,0:T(8,128)} copy(f32[7,1,16,128]{3,2,1,0:T(8,128)} %collective-permute-done.1) | data formatting | bytes 114688 | tf_op jit(solution)/shard_map/ppermute | solution.py:42
  69.0 2.4 %pad_maximum_fusion.33 = (f32[7,98,1,128]{1,3,2,0:T(8,128)S(1)}, f32[7,98,1,128]{1,3,2,0:T(8,128)S(1)}) fusion(f32[7,1,16,128]{1,3,2,0:T(8,128)} %copy.29, f32[7,96,16,128]{1,3,2,0:T(8,128)} %copy.27, f32[7,1,16,128]{1,3,2,0:T(8,128)} %copy.30), kind=kLoop, calls=%fused_computation.92 | loop fusion | flops 351232 | bytes 6322176 | tf_op jit(solution)/shard_map/concatenate | solution.py:46
  71.4 1.6 collective-permute-start.2
  73.0 3.1 %collective-permute-start.3 = (f32[7,98,1,128]{1,3,2,0:T(8,128)S(1)}, f32[7,98,1,128]{1,3,2,0:T(8,128)S(1)}, u32[]{:S(2)}, u32[]{:S(2)}) collective-permute-start(f32[7,98,1,128]{1,3,2,0:T(8,128)S(1)} %get-tuple-element.16), channel_id=1, source_target_pairs={{0,4},{1,5},{2,6},{3,7},{8,12},{9,13},{10,14},{11,15},{16,20},{17,... | collective-permute-start | bytes 1053704 | tf_op jit(solution)/shard_map/ppermute | solution.py:42
  76.1 1.1 fusion.40
  77.5 1.9 pad_maximum_fusion.39
  79.4 1.3 collective-permute-start.4
  80.7 4.7 %collective-permute-start.5 = (f32[7,98,18,1]{1,3,2,0:T(1,128)S(1)}, f32[7,98,18,1]{1,3,2,0:T(1,128)S(1)}, u32[]{:S(2)}, u32[]{:S(2)}) collective-permute-start(f32[7,98,18,1]{1,3,2,0:T(1,128)S(1)} %get-tuple-element.14), channel_id=1, source_target_pairs={{0,1},{1,2},{2,3},{4,5},{5,6},{6,7},{8,9},{9,10},{10,11},{12,13},{... | collective-permute-start | bytes 148184 | tf_op jit(solution)/shard_map/ppermute | solution.py:42
  85.4 0.8 fusion.44
  86.2 0.9 collective-permute-done.5
  87.1 47.5 %fusion.62 = (f32[96,16,128]{0,2,1:T(8,128)S(1)}, f32[6,96,16,128]{1,3,2,0:T(8,128)}) fusion(f32[96,16,128]{0,2,1:T(8,128)} %fusion.40, f32[6]{0:T(128)} %constant.109.clone, f32[7,98,1,128]{1,3,2,0:T(8,128)} %copy-done.3, f32[7,1,16,128]{1,3,2,0:T(8,128)} %copy.29, f32[7,96,16,128]{1,3,2,0:T(8,128)} %copy.27, f32[7,1,16,128]{1,3,2,0:T(8,128)} %copy.30, ...), kind=kLoop, calls=%fused_computation.226 | loop fusion | flops 38731776 | bytes 35881976 | tf_op jit(solution)/shard_map/reduce_sum | solution.py:136
  135.4 1.7 collective-permute-start.6
  137.4 1.3 collective-permute-start.7
  138.7 0.7 slice_reduce_fusion.1
  139.7 4.3 %collective-permute-done.7 = f32[1,16,128]{2,1,0:T(8,128)S(1)} collective-permute-done((f32[1,16,128]{2,1,0:T(8,128)S(1)}, f32[1,16,128]{2,1,0:T(8,128)S(1)}, u32[]{:S(2)}, u32[]{:S(2)}) %collective-permute-start.7) | collective-permute-done | bytes 8224 | tf_op jit(solution)/shard_map/ppermute | solution.py:45
  144.6 1.4 collective-permute-start.8
  146.0 1.3 collective-permute-start.9
  147.4 0.9 pad_maximum_fusion.47
  148.2 1.3 collective-permute-start.14
  149.5 4.9 %collective-permute-start.15 = (f32[96,18,1]{0,2,1:T(1,128)S(1)}, f32[96,18,1]{0,2,1:T(1,128)S(1)}, u32[]{:S(2)}, u32[]{:S(2)}) collective-permute-start(f32[96,18,1]{0,2,1:T(1,128)S(1)} %get-tuple-element.25), channel_id=1, source_target_pairs={{0,1},{1,2},{2,3},{4,5},{5,6},{6,7},{8,9},{9,10},{10,11},{12,13},{... | collective-permute-start | bytes 20744 | tf_op jit(solution)/shard_map/ppermute | solution.py:42
  154.6 3.9 %collective-permute-start.10 = (f32[98,18,1]{0,2,1:T(1,128)S(1)}, f32[98,18,1]{0,2,1:T(1,128)S(1)}, u32[]{:S(2)}, u32[]{:S(2)}) collective-permute-start(f32[98,18,1]{0,2,1:T(1,128)S(1)} %get-tuple-element.20), channel_id=1, source_target_pairs={{0,1},{1,2},{2,3},{4,5},{5,6},{6,7},{8,9},{9,10},{10,11},{12,13},{... | collective-permute-start | bytes 21176 | tf_op jit(solution)/shard_map/ppermute | solution.py:42
  158.6 1.6 collective-permute-start.11
  160.2 2.5 %fusion.10 = f32[98,18,130]{0,2,1:T(8,128)S(1)} fusion(f32[7,98,18,1]{1,3,2,0:T(1,128)S(1)} %collective-permute-done.4, f32[7,98,18,1]{1,3,2,0:T(1,128)S(1)} %collective-permute-done.5, f32[7,98,1,128]{1,3,2,0:T(8,128)S(1)} %copy-done.4, f32[7,98,1,128]{1,3,2,0:T(8,128)S(1)} %copy-done.6, f32[7,1,16,128]{1,3,2,0:T(8,128)} %copy.29, ...), kind=kLoop, calls=%fused_computation.32 | loop fusion | flops 1375920 | bytes 7338240 | tf_op jit(solution)/shard_map/squeeze | solution.py:138
  162.8 1.5 collective-permute-done.11
  165.0 6.4 %fusion.16 = (f32[96,16,128]{0,2,1:T(8,128)S(1)}, f32[96,16,128]{0,2,1:T(8,128)S(1)}) fusion(f32[96,16,128]{0,2,1:T(8,128)S(1)} %copy-done.2, f32[96,18,1]{0,2,1:T(1,128)S(1)} %collective-permute-done.15, f32[96,1,128]{0,2,1:T(8,128)S(1)} %collective-permute-done.12, f32[96,1,128]{0,2,1:T(8,128)S(1)} %collective-permute-done.13, ...), kind=kLoop, calls=%fused_computation.45 | loop fusion | flops 10813440 | bytes 15078912 | tf_op jit(solution)/shard_map/add | solution.py:98
  171.3 1.2 convolution_bitcast_fusion
  172.7 3.0 %collective-permute-start.16 = (f32[2,2048]{1,0:T(2,128)S(1)}, f32[2,2048]{1,0:T(2,128)S(1)}, u32[]{:S(2)}, u32[]{:S(2)}) collective-permute-start(f32[2,2048]{1,0:T(2,128)S(1)} %get-tuple-element.38), channel_id=1, source_target_pairs={{0,8},{8,16},{16,24},{24,0},{1,9},{9,17},{17,25},{25,1},{2,10},{10... | collective-permute-start | bytes 49160 | tf_op jit(solution)/shard_map/ppermute | solution.py:27
  175.6 3.8 %pad_maximum_fusion = f32[7,96,16,128]{1,3,2,0:T(8,128)} fusion(f32[1,96,16,128]{1,3,2,0:T(8,128)S(1)} %bitcast.73, f32[6,96,16,128]{1,3,2,0:T(8,128)S(1)} %bitcast.72), kind=kLoop, calls=%fused_computation.1 | loop fusion | flops 1376256 | bytes 11010048 | tf_op jit(solution)/shard_map/concatenate | solution.py:140
  179.4 7.9 %copy.49 = f32[7,96,16,128]{3,2,1,0:T(8,128)} copy(f32[7,96,16,128]{1,3,2,0:T(8,128)} %pad_maximum_fusion) | data formatting | bytes 11010048
  187.4 2.0 %collective-permute-start.18 = (f32[2,2048]{1,0:T(2,128)S(1)}, f32[2,2048]{1,0:T(2,128)S(1)}, u32[]{:S(2)}, u32[]{:S(2)}) collective-permute-start(f32[2,2048]{1,0:T(2,128)S(1)} %collective-permute-done.16), channel_id=1, source_target_pairs={{0,8},{8,16},{16,24},{24,0},{1,9},{9,17},{17,25},{25,1},{2,10},{10... | collective-permute-start | bytes 49160 | tf_op jit(solution)/shard_map/ppermute | solution.py:27
  189.4 2.6 %collective-permute-done.18 = f32[2,2048]{1,0:T(2,128)S(1)} collective-permute-done((f32[2,2048]{1,0:T(2,128)S(1)}, f32[2,2048]{1,0:T(2,128)S(1)}, u32[]{:S(2)}, u32[]{:S(2)}) %collective-permute-start.18) | collective-permute-done | bytes 16416 | tf_op jit(solution)/shard_map/ppermute | solution.py:27
  192.2 1.2 slice_multiply_fusion.3
  193.6 1.0 copy.50
  (142 shorter events, 21.8 us)
Async XLA Ops:
  1.5 57.8 %collective-permute-start = (f32[7,1,16,128]{3,2,1,0:T(8,128)S(1)}, f32[7,1,16,128]{3,2,1,0:T(8,128)S(1)}, u32[]{:S(2)}, u32[]{:S(2)}) collective-permute-start(f32[7,1,16,128]{3,2,1,0:T(8,128)S(1)} %get-tuple-element.19), channel_id=1, source_target_pairs={{8,0},{16,8},{24,16},{9,1},{17,9},{25,17},{10,2},{18,10},{26,18},{... | collective-permute-start | bytes 172040 | tf_op jit(solution)/shard_map/ppermute | solution.py:45
  2.8 61.0 %collective-permute-start.1 = (f32[7,1,16,128]{3,2,1,0:T(8,128)S(1)}, f32[7,1,16,128]{3,2,1,0:T(8,128)}, u32[]{:S(2)}, u32[]{:S(2)}) collective-permute-start(f32[7,1,16,128]{3,2,1,0:T(8,128)S(1)} %get-tuple-element.18), channel_id=1, source_target_pairs={{0,8},{8,16},{16,24},{1,9},{9,17},{17,25},{2,10},{10,18},{18,26},{... | collective-permute-start | bytes 172040 | tf_op jit(solution)/shard_map/ppermute | solution.py:42
  10.4 13.1 %copy-start.1 = (f32[96,16,128]{0,2,1:T(8,128)}, f32[96,16,128]{0,2,1:T(8,128)S(1)}, u32[]{:S(2)}) copy-start(f32[96,16,128]{0,2,1:T(8,128)S(1)} %copy.47) | copy-start | bytes 2359300
  11.1 136.3 %collective-permute-start.12 = (f32[96,1,128]{0,2,1:T(8,128)}, f32[96,1,128]{0,2,1:T(8,128)S(1)}, u32[]{:S(2)}, u32[]{:S(2)}) collective-permute-start(f32[96,1,128]{0,2,1:T(8,128)} %get-tuple-element.29), channel_id=1, source_target_pairs={{4,0},{5,1},{6,2},{7,3},{12,8},{13,9},{14,10},{15,11},{20,16},{21,... | collective-permute-start | bytes 147464 | tf_op jit(solution)/shard_map/ppermute | solution.py:45
  12.3 11.4 %copy-start.9 = (s32[16,128]{1,0:T(8,128)S(1)}, s32[16,128]{1,0:T(8,128)}, u32[]{:S(2)}) copy-start(s32[16,128]{1,0:T(8,128)} %param.11) | copy-start | bytes 24580
  12.4 11.4 %copy-start.7 = (f32[96,96]{1,0:T(8,128)S(1)}, f32[96,96]{1,0:T(8,128)}, u32[]{:S(2)}) copy-start(f32[96,96]{1,0:T(8,128)} %param.12) | copy-start | bytes 110596
  12.4 12.0 %copy-start.12 = (f32[1,2]{1,0:T(1,128)S(1)}, f32[1,2]{1,0:T(1,128)}, u32[]{:S(2)}) copy-start(f32[1,2]{1,0:T(1,128)} %param.13) | copy-start | bytes 28
  12.4 12.6 %copy-start.15 = (u32[32]{0:T(128)S(1)}, u32[32]{0:T(128)}, u32[]{:S(2)}) copy-start(u32[32]{0:T(128)} %constant.113) | copy-start | bytes 388
  12.4 135.0 %collective-permute-start.13 = (f32[96,1,128]{0,2,1:T(8,128)S(1)}, f32[96,1,128]{0,2,1:T(8,128)S(1)}, u32[]{:S(2)}, u32[]{:S(2)}) collective-permute-start(f32[96,1,128]{0,2,1:T(8,128)S(1)} %get-tuple-element.28), channel_id=1, source_target_pairs={{0,4},{1,5},{2,6},{3,7},{8,12},{9,13},{10,14},{11,15},{16,20},{17,... | collective-permute-start | bytes 147464 | tf_op jit(solution)/shard_map/ppermute | solution.py:42
  63.8 12.3 %slice-start = ((s8[7340032]{0:T(1024)(128)(4,1)}), s8[3145728]{0:T(1024)(128)(4,1)S(1)}, s32[]{:S(2)}) async-start(s8[7340032]{0:T(1024)(128)(4,1)} %bitcast.69), calls=%async_computation | async-start | bytes 6291456
  69.0 7.1 %slice-start.1 = ((s8[7340032]{0:T(1024)(128)(4,1)}), s8[4194304]{0:T(1024)(128)(4,1)S(1)}, s32[]{:S(2)}) async-start(s8[7340032]{0:T(1024)(128)(4,1)} %bitcast.69), calls=%async_computation.1 | async-start | bytes 8388608
  69.0 8.5 %copy-start = (f32[7,1,16,128]{1,3,2,0:T(8,128)S(1)}, f32[7,1,16,128]{1,3,2,0:T(8,128)}, u32[]{:S(2)}) copy-start(f32[7,1,16,128]{1,3,2,0:T(8,128)} %copy.30) | copy-start | bytes 172036
  71.4 5.8 %collective-permute-start.2 = (f32[7,98,1,128]{1,3,2,0:T(8,128)S(1)}, f32[7,98,1,128]{1,3,2,0:T(8,128)S(1)}, u32[]{:S(2)}, u32[]{:S(2)}) collective-permute-start(f32[7,98,1,128]{1,3,2,0:T(8,128)S(1)} %get-tuple-element.17), channel_id=1, source_target_pairs={{4,0},{5,1},{6,2},{7,3},{12,8},{13,9},{14,10},{15,11},{20,16},{21,... | collective-permute-start | bytes 1053704 | tf_op jit(solution)/shard_map/ppermute | solution.py:45
  73.0 4.5 %collective-permute-start.3 = (f32[7,98,1,128]{1,3,2,0:T(8,128)S(1)}, f32[7,98,1,128]{1,3,2,0:T(8,128)S(1)}, u32[]{:S(2)}, u32[]{:S(2)}) collective-permute-start(f32[7,98,1,128]{1,3,2,0:T(8,128)S(1)} %get-tuple-element.16), channel_id=1, source_target_pairs={{0,4},{1,5},{2,6},{3,7},{8,12},{9,13},{10,14},{11,15},{16,20},{17,... | collective-permute-start | bytes 1053704 | tf_op jit(solution)/shard_map/ppermute | solution.py:42
  77.2 8.2 %copy-start.16 = (f32[8]{0:T(128)S(1)}, f32[8]{0:T(128)}, u32[]{:S(2)}) copy-start(f32[8]{0:T(128)} %divide_bitcast_fusion.1) | copy-start | bytes 100
  77.2 9.9 %copy-start.14 = (f32[6]{0:T(128)S(1)}, f32[6]{0:T(128)}, u32[]{:S(2)}) copy-start(f32[6]{0:T(128)} %constant.108.clone) | copy-start | bytes 76
  77.2 2.1 %copy-start.3 = (f32[7,98,1,128]{1,3,2,0:T(8,128)}, f32[7,98,1,128]{1,3,2,0:T(8,128)S(1)}, u32[]{:S(2)}) copy-start(f32[7,98,1,128]{1,3,2,0:T(8,128)S(1)} %collective-permute-done.2) | copy-start | bytes 1053700
  77.5 1.9 copy-start.5
  79.4 6.9 %collective-permute-start.4 = (f32[7,98,18,1]{1,3,2,0:T(1,128)S(1)}, f32[7,98,18,1]{1,3,2,0:T(1,128)S(1)}, u32[]{:S(2)}, u32[]{:S(2)}) collective-permute-start(f32[7,98,18,1]{1,3,2,0:T(1,128)S(1)} %get-tuple-element.15), channel_id=1, source_target_pairs={{1,0},{2,1},{3,2},{5,4},{6,5},{7,6},{9,8},{10,9},{11,10},{13,12},{... | collective-permute-start | bytes 148184 | tf_op jit(solution)/shard_map/ppermute | solution.py:45
  80.7 6.4 %collective-permute-start.5 = (f32[7,98,18,1]{1,3,2,0:T(1,128)S(1)}, f32[7,98,18,1]{1,3,2,0:T(1,128)S(1)}, u32[]{:S(2)}, u32[]{:S(2)}) collective-permute-start(f32[7,98,18,1]{1,3,2,0:T(1,128)S(1)} %get-tuple-element.14), channel_id=1, source_target_pairs={{0,1},{1,2},{2,3},{4,5},{5,6},{6,7},{8,9},{9,10},{10,11},{12,13},{... | collective-permute-start | bytes 148184 | tf_op jit(solution)/shard_map/ppermute | solution.py:42
  135.4 4.0 %collective-permute-start.6 = (f32[1,16,128]{2,1,0:T(8,128)S(1)}, f32[1,16,128]{2,1,0:T(8,128)S(1)}, u32[]{:S(2)}, u32[]{:S(2)}) collective-permute-start(f32[1,16,128]{2,1,0:T(8,128)S(1)} %copy.37), channel_id=1, source_target_pairs={{0,8},{8,16},{16,24},{1,9},{9,17},{17,25},{2,10},{10,18},{18,26},{... | collective-permute-start | bytes 24584 | tf_op jit(solution)/shard_map/ppermute | solution.py:42
  137.4 6.7 %collective-permute-start.7 = (f32[1,16,128]{2,1,0:T(8,128)S(1)}, f32[1,16,128]{2,1,0:T(8,128)S(1)}, u32[]{:S(2)}, u32[]{:S(2)}) collective-permute-start(f32[1,16,128]{2,1,0:T(8,128)S(1)} %copy.38), channel_id=1, source_target_pairs={{8,0},{16,8},{24,16},{9,1},{17,9},{25,17},{10,2},{18,10},{26,18},{... | collective-permute-start | bytes 24584 | tf_op jit(solution)/shard_map/ppermute | solution.py:45
  144.4 15.8 %copy-start.4 = (f32[7,98,1,128]{1,3,2,0:T(8,128)S(1)}, f32[7,98,1,128]{1,3,2,0:T(8,128)}, u32[]{:S(2)}) copy-start(f32[7,98,1,128]{1,3,2,0:T(8,128)} %copy-done.3) | copy-start | bytes 1053700
  144.4 15.8 %copy-start.6 = (f32[7,98,1,128]{1,3,2,0:T(8,128)S(1)}, f32[7,98,1,128]{1,3,2,0:T(8,128)}, u32[]{:S(2)}) copy-start(f32[7,98,1,128]{1,3,2,0:T(8,128)} %copy-done.5) | copy-start | bytes 1053700
  144.6 9.9 %collective-permute-start.8 = (f32[98,1,128]{0,2,1:T(8,128)S(1)}, f32[98,1,128]{0,2,1:T(8,128)S(1)}, u32[]{:S(2)}, u32[]{:S(2)}) collective-permute-start(f32[98,1,128]{0,2,1:T(8,128)S(1)} %get-tuple-element.22), channel_id=1, source_target_pairs={{0,4},{1,5},{2,6},{3,7},{8,12},{9,13},{10,14},{11,15},{16,20},{17,... | collective-permute-start | bytes 150536 | tf_op jit(solution)/shard_map/ppermute | solution.py:42
  146.0 8.4 %collective-permute-start.9 = (f32[98,1,128]{0,2,1:T(8,128)S(1)}, f32[98,1,128]{0,2,1:T(8,128)S(1)}, u32[]{:S(2)}, u32[]{:S(2)}) collective-permute-start(f32[98,1,128]{0,2,1:T(8,128)S(1)} %get-tuple-element.23), channel_id=1, source_target_pairs={{4,0},{5,1},{6,2},{7,3},{12,8},{13,9},{14,10},{15,11},{20,16},{21,... | collective-permute-start | bytes 150536 | tf_op jit(solution)/shard_map/ppermute | solution.py:45
  148.2 16.7 %collective-permute-start.14 = (f32[96,18,1]{0,2,1:T(1,128)S(1)}, f32[96,18,1]{0,2,1:T(1,128)S(1)}, u32[]{:S(2)}, u32[]{:S(2)}) collective-permute-start(f32[96,18,1]{0,2,1:T(1,128)S(1)} %get-tuple-element.24), channel_id=1, source_target_pairs={{1,0},{2,1},{3,2},{5,4},{6,5},{7,6},{9,8},{10,9},{11,10},{13,12},{... | collective-permute-start | bytes 20744 | tf_op jit(solution)/shard_map/ppermute | solution.py:45
  149.5 15.4 %collective-permute-start.15 = (f32[96,18,1]{0,2,1:T(1,128)S(1)}, f32[96,18,1]{0,2,1:T(1,128)S(1)}, u32[]{:S(2)}, u32[]{:S(2)}) collective-permute-start(f32[96,18,1]{0,2,1:T(1,128)S(1)} %get-tuple-element.25), channel_id=1, source_target_pairs={{0,1},{1,2},{2,3},{4,5},{5,6},{6,7},{8,9},{9,10},{10,11},{12,13},{... | collective-permute-start | bytes 20744 | tf_op jit(solution)/shard_map/ppermute | solution.py:42
  154.6 8.1 %collective-permute-start.10 = (f32[98,18,1]{0,2,1:T(1,128)S(1)}, f32[98,18,1]{0,2,1:T(1,128)S(1)}, u32[]{:S(2)}, u32[]{:S(2)}) collective-permute-start(f32[98,18,1]{0,2,1:T(1,128)S(1)} %get-tuple-element.20), channel_id=1, source_target_pairs={{0,1},{1,2},{2,3},{4,5},{5,6},{6,7},{8,9},{9,10},{10,11},{12,13},{... | collective-permute-start | bytes 21176 | tf_op jit(solution)/shard_map/ppermute | solution.py:42
  158.5 6.4 %copy-start.2 = (f32[96,16,128]{0,2,1:T(8,128)S(1)}, f32[96,16,128]{0,2,1:T(8,128)}, u32[]{:S(2)}) copy-start(f32[96,16,128]{0,2,1:T(8,128)} %copy-done.1) | copy-start | bytes 2359300
  158.6 6.4 %copy-start.8 = (f32[16,128]{1,0:T(8,128)S(1)}, f32[16,128]{1,0:T(8,128)}, u32[]{:S(2)}) copy-start(f32[16,128]{1,0:T(8,128)} %param.10) | copy-start | bytes 24580
  158.6 5.7 %collective-permute-start.11 = (f32[98,18,1]{0,2,1:T(1,128)S(1)}, f32[98,18,1]{0,2,1:T(1,128)S(1)}, u32[]{:S(2)}, u32[]{:S(2)}) collective-permute-start(f32[98,18,1]{0,2,1:T(1,128)S(1)} %get-tuple-element.21), channel_id=1, source_target_pairs={{1,0},{2,1},{3,2},{5,4},{6,5},{7,6},{9,8},{10,9},{11,10},{13,12},{... | collective-permute-start | bytes 21176 | tf_op jit(solution)/shard_map/ppermute | solution.py:45
  164.9 10.7 %slice-start.2 = ((s8[6291456]{0:T(1024)(128)(4,1)}), s8[4194304]{0:T(1024)(128)(4,1)S(1)}, s32[]{:S(2)}) async-start(s8[6291456]{0:T(1024)(128)(4,1)} %bitcast.71), calls=%async_computation.2 | async-start | bytes 8388608
  165.0 10.7 %slice-start.3 = ((s8[6291456]{0:T(1024)(128)(4,1)}), s8[2097152]{0:T(1024)(128)(4,1)S(1)}, s32[]{:S(2)}) async-start(s8[6291456]{0:T(1024)(128)(4,1)} %bitcast.71), calls=%async_computation.3 | async-start | bytes 4194304
  172.7 14.7 %collective-permute-start.16 = (f32[2,2048]{1,0:T(2,128)S(1)}, f32[2,2048]{1,0:T(2,128)S(1)}, u32[]{:S(2)}, u32[]{:S(2)}) collective-permute-start(f32[2,2048]{1,0:T(2,128)S(1)} %get-tuple-element.38), channel_id=1, source_target_pairs={{0,8},{8,16},{16,24},{24,0},{1,9},{9,17},{17,25},{25,1},{2,10},{10... | collective-permute-start | bytes 49160 | tf_op jit(solution)/shard_map/ppermute | solution.py:27
  175.6 13.8 %collective-permute-start.17 = (f32[2,2048]{1,0:T(2,128)S(1)}, f32[2,2048]{1,0:T(2,128)S(1)}, u32[]{:S(2)}, u32[]{:S(2)}) collective-permute-start(f32[2,2048]{1,0:T(2,128)S(1)} %get-tuple-element.38), channel_id=1, source_target_pairs={{0,24},{8,0},{16,8},{24,16},{1,25},{9,1},{17,9},{25,17},{2,26},{10... | collective-permute-start | bytes 49160 | tf_op jit(solution)/shard_map/ppermute | solution.py:30
  179.4 12.6 %copy-start.13 = (f32[2,8]{1,0:T(2,128)S(1)}, f32[2,8]{1,0:T(2,128)}, u32[]{:S(2)}) copy-start(f32[2,8]{1,0:T(2,128)} %fusion.44) | copy-start | bytes 196
  179.4 13.9 %copy-start.10 = (f32[96]{0:T(128)S(1)}, f32[96]{0:T(128)}, u32[]{:S(2)}) copy-start(f32[96]{0:T(128)} %get-tuple-element.6) | copy-start | bytes 1156
  179.4 14.0 %copy-start.11 = (f32[96]{0:T(128)S(1)}, f32[96]{0:T(128)}, u32[]{:S(2)}) copy-start(f32[96]{0:T(128)} %get-tuple-element.7) | copy-start | bytes 1156
  187.4 4.6 %collective-permute-start.18 = (f32[2,2048]{1,0:T(2,128)S(1)}, f32[2,2048]{1,0:T(2,128)S(1)}, u32[]{:S(2)}, u32[]{:S(2)}) collective-permute-start(f32[2,2048]{1,0:T(2,128)S(1)} %collective-permute-done.16), channel_id=1, source_target_pairs={{0,8},{8,16},{16,24},{24,0},{1,9},{9,17},{17,25},{25,1},{2,10},{10... | collective-permute-start | bytes 49160 | tf_op jit(solution)/shard_map/ppermute | solution.py:27
